TPU v7x, 256 devices: a whole 4x4x8 slice. The times are simulated.
256 devices in a mesh: row: 32 (over y, x, core), col: 8 (over z).
Axes of the slice: x: 4, y: 4, z: 8, core: 2. Of those that a mesh axis runs over, the one named last changes fastest.
Arguments:
- inputs: bfloat16 [768, 12288], P(None, 'col'), may hold values from -6 to 6
- out_grad: bfloat16 [768, 12288], P(None, 'col'), may hold values from -6 to 6
- pre_act: bfloat16 [768, 24576], P('col', 'row'), may hold values from -8 to 8
- w_in: bfloat16 [12288, 24576], P('col', 'row'), may hold values from -0.0546875 to 0.0546875
- w_out: bfloat16 [24576, 12288], P('row', 'col'), may hold values from -0.0390625 to 0.0390625
Outputs:
- grad_inputs: bfloat16 [768, 12288], P('row', 'col')
- grad_w_in: bfloat16 [12288, 24576], P('col', 'row')
- grad_w_out: bfloat16 [24576, 12288], P('row', 'col')
All inputs are finite; a program needn't handle non-finite values.
Results may differ from a plain program's by a relative error of at most 0.0049.
Values may be sent and summed in bfloat16 or wider, within the bound.
A program may use at most 64 MiB of HBM per device.

v0:
```python
import math
import jax
import jax.numpy as jnp
from jax import lax
from jax.sharding import PartitionSpec as P

coef_c = math.sqrt(2.0 / math.pi)


def gelu_parts(pre_values):
    hval = pre_values.astype(jnp.float32)
    tval = jnp.tanh(coef_c * (hval + 0.044715 * hval * hval * hval))
    activ = 0.5 * hval * (1.0 + tval)
    deriv = 0.5 * (1.0 + tval) + 0.5 * hval * (1.0 - tval * tval) * coef_c * (
        1.0 + 3.0 * 0.044715 * hval * hval
    )
    return (activ, deriv)


def per_device(inputs, out_grad, pre_act, w_in, w_out):
    total_tokens = inputs.shape[0]
    scale_value = 1.0 / math.sqrt(total_tokens)
    block = out_grad
    act_share = lax.psum_scatter(
        lax.dot_general(block, w_out, (((1,), (1,)), ((), ())), preferred_element_type=jnp.float32),
        "col",
        scatter_dimension=0,
        tiled=True,
    )
    local_act, local_deriv = gelu_parts(pre_act)
    hid_share = (act_share * local_deriv).astype(jnp.bfloat16)
    activ_all, hid_all = (
        lax.all_gather(local_act.astype(jnp.bfloat16), "col", axis=0, tiled=True),
        lax.all_gather(hid_share, "col", axis=0, tiled=True),
    )
    grad_w_out = lax.dot_general(
        activ_all, out_grad, (((0,), (0,)), ((), ())), preferred_element_type=jnp.float32
    )
    grad_w_out = (grad_w_out * scale_value).astype(jnp.bfloat16)
    grad_w_in = lax.dot_general(
        inputs, hid_all, (((0,), (0,)), ((), ())), preferred_element_type=jnp.float32
    )
    grad_w_in = (grad_w_in * scale_value).astype(jnp.bfloat16)
    block = hid_all
    grad_inputs = lax.psum_scatter(
        lax.dot_general(block, w_in, (((1,), (1,)), ((), ())), preferred_element_type=jnp.float32),
        "row",
        scatter_dimension=0,
        tiled=True,
    )
    return (grad_inputs.astype(jnp.bfloat16), grad_w_in, grad_w_out)


def solution(mesh):
    placed = (P(None, "col"), P(None, "col"), P("col", "row"), P("col", "row"), P("row", "col"))
    return jax.shard_map(
        per_device,
        mesh=mesh,
        in_specs=placed,
        out_specs=(P("row", "col"), P("col", "row"), P("row", "col")),
        check_vma=False,
    )
```

profile of v0, /device:TPU:2, one launch (start us, length us, event | category | flops | bytes accessed | tf_op | source)
XLA Modules:
  0.0 241.4 jit_solution(5547403851123938522)
XLA Ops:
  7.2 0.0 copy-start
  7.2 0.0 reduce-scatter.3.cloned.1.call-start
  7.2 1.6 copy-done
  8.8 5.1 %fusion.12 = f32[768,768]{1,0:T(8,128)} fusion(bf16[768,1536]{1,0:T(8,128)(2,1)S(1)} %copy-done, bf16[768,1536]{1,0:T(8,128)(2,1)} %param.9), kind=kOutput, calls=%fused_computation.21 | convolution fusion | flops 1811939328 | bytes 7077888 | tf_op jit(solution)/shard_map/dot_general | solution.py:25
  13.9 0.0 copy-start.1
  13.9 0.0 reduce-scatter.3.cloned.1.call-update
  13.9 0.0 all-gather.3.cloned.1.call-start
  14.0 46.3 %reduce-scatter.3.cloned.1.call-done = f32[96,768]{1,0:T(8,128)} async-done(((f32[768,768]{1,0:T(8,128)}), f32[96,768]{1,0:T(8,128)}) %reduce-scatter.3.cloned.1.call-update) | async-done | bytes 294928 | tf_op jit(solution)/shard_map/reduce_scatter | solution.py:24
  60.3 0.0 copy-done.1
  60.3 1.9 fusion.8
  62.1 0.0 all-gather.3.cloned.1.call-update
  62.2 0.0 all-gather.5.cloned.1.call-start
  62.2 0.7 all-gather.5.cloned.1.call-update
  62.9 0.0 reduce-scatter.5.cloned.1.call-start
  63.0 37.7 %all-gather.3.cloned.1.call-done = bf16[768,768]{1,0:T(8,128)(2,1)} async-done(((bf16[96,768]{1,0:T(8,128)(2,1)}), bf16[768,768]{1,0:T(8,128)(2,1)}) %all-gather.3.cloned.1.call-update) | async-done | bytes 1179664 | tf_op jit(solution)/shard_map/all_gather | solution.py:34
  100.7 6.2 %fusion.13 = f32[768,1536]{1,0:T(8,128)} fusion(bf16[768,768]{1,0:T(8,128)(2,1)} %all-gather.3.cloned.1.call-done, bf16[1536,768]{1,0:T(8,128)(2,1)} %param.8), kind=kOutput, calls=%fused_computation.22 | convolution fusion | flops 1811939328 | bytes 8257536 | tf_op jit(solution)/shard_map/dot_general | solution.py:46
  106.9 0.0 copy-start.2
  106.9 0.0 reduce-scatter.5.cloned.1.call-update
  106.9 1.2 copy-done.2
  108.1 5.1 %fusion = bf16[1536,768]{0,1:T(8,128)(2,1)} fusion(bf16[768,768]{1,0:T(8,128)(2,1)S(1)} %copy-done.2, bf16[768,1536]{1,0:T(8,128)(2,1)} %param.5), kind=kOutput, calls=%fused_computation.2 | convolution fusion | flops 1814298624 | bytes 5898240 | tf_op jit(solution)/shard_map/dot_general | solution.py:40
  113.2 4.3 %copy.8 = bf16[1536,768]{1,0:T(8,128)(2,1)} copy(bf16[1536,768]{0,1:T(8,128)(2,1)} %fusion) | data formatting | bytes 4718592
  117.5 22.2 %all-gather.5.cloned.1.call-done = bf16[768,768]{1,0:T(8,128)(2,1)} async-done(((bf16[96,768]{1,0:T(8,128)(2,1)}), bf16[768,768]{1,0:T(8,128)(2,1)}) %all-gather.5.cloned.1.call-update) | async-done | bytes 1179664 | tf_op jit(solution)/shard_map/all_gather | solution.py:33
  139.7 4.7 %multiply_convert_fusion = bf16[768,1536]{1,0:T(8,128)(2,1)} fusion(bf16[768,768]{1,0:T(8,128)(2,1)} %all-gather.5.cloned.1.call-done, bf16[768,1536]{1,0:T(8,128)(2,1)S(1)} %copy-done), kind=kOutput, calls=%fused_computation | convolution fusion | flops 1814298624 | bytes 5898240 | tf_op jit(solution)/shard_map/dot_general | solution.py:36
  144.4 88.9 %reduce-scatter.5.cloned.1.call-done = f32[24,1536]{1,0:T(8,128)} async-done(((f32[768,1536]{1,0:T(8,128)}), f32[24,1536]{1,0:T(8,128)}) %reduce-scatter.5.cloned.1.call-update) | async-done | bytes 147472 | tf_op jit(solution)/shard_map/reduce_scatter | solution.py:45
  233.3 1.6 convert_element_type.23
Async XLA Ops:
  7.2 1.7 copy-start
  7.2 53.1 %reduce-scatter.3.cloned.1.call-start = ((), (), s32[]{:S(2)}) async-start(), calls=%async_computation.2 | async-start | bytes 2654208 | tf_op jit(solution)/shard_map/reduce_scatter | solution.py:24
  13.9 46.3 %copy-start.1 = (bf16[96,768]{1,0:T(8,128)(2,1)S(1)}, bf16[96,768]{1,0:T(8,128)(2,1)}, u32[]{:S(2)}) copy-start(bf16[96,768]{1,0:T(8,128)(2,1)} %param.7) | copy-start | bytes 442372
  13.9 86.7 %all-gather.3.cloned.1.call-start = ((), (), s32[]{:S(2)}) async-start(), calls=%async_computation.3 | async-start | bytes 1327104 | tf_op jit(solution)/shard_map/all_gather | solution.py:34
  62.2 77.6 %all-gather.5.cloned.1.call-start = ((), (), s32[]{:S(2)}) async-start(), calls=%async_computation.5 | async-start | bytes 1327104 | tf_op jit(solution)/shard_map/all_gather | solution.py:33
  62.9 170.4 %reduce-scatter.5.cloned.1.call-start = ((), (), s32[]{:S(2)}) async-start(), calls=%async_computation.4 | async-start | bytes 4866048 | tf_op jit(solution)/shard_map/reduce_scatter | solution.py:45
  106.9 1.3 copy-start.2
Sparse Core Ops, SparseCore 0:
  14.1 46.1 reduce-scatter.2
  62.6 37.9 all-gather.2
  102.5 37.2 all-gather.4
  143.6 89.6 reduce-scatter.4
where the time goes:
time: 242 us; the launch traced here: 241 us
  waiting for transfers between devices  196 us (81%)
  matrix products  21.1 us (9%)
  between operations  13.8 us (6%)
  local copies, waits for them, and re-layouts  7.13 us (3%)
  other arithmetic  3.43 us (1%)
    reduce_scatter x1, waiting for transfers between devices, per_device(): lax.psum_scatter(lax.dot_general(block, w_in, (((1,), (1,)), ((), ())), p...  88.9 us
    reduce_scatter x1, waiting for transfers between devices, per_device(): lax.psum_scatter(lax.dot_general(block, w_out, (((1,), (1,)), ((), ())),...  46.3 us
    all_gather x1, waiting for transfers between devices, per_device(): lax.all_gather(hid_share, 'col', axis=0, tiled=True)  37.7 us
    all_gather x1, waiting for transfers between devices, per_device(): lax.all_gather(local_act.astype(jnp.bfloat16), 'col', axis=0, tiled=True)  22.2 us
    unnamed x7, local copies, waits for them, and re-layouts  7.13 us
    dot_general x1, matrix products, per_device(): lax.dot_general(block, w_in, (((1,), (1,)), ((), ())), preferred_element_...  6.2 us
    dot_general x1, matrix products, per_device(): lax.dot_general(inputs, hid_all, (((0,), (0,)), ((), ())), preferred_elem...  5.1 us
    dot_general x1, matrix products, per_device(): lax.dot_general(block, w_out, (((1,), (1,)), ((), ())), preferred_element...  5.09 us
  transfers between devices with their start and end apart: 4, of which 4 were waited for; matrix products, arithmetic and copies ran while one was open for 8% of the time, Pallas kernels for 0%

commit v1 on v0

--- a/solution.py
+++ b/solution.py
@@ -31,7 +31,9 @@
     hid_share = (act_share * local_deriv).astype(jnp.bfloat16)
     activ_all, hid_all = (
         lax.all_gather(local_act.astype(jnp.bfloat16), "col", axis=0, tiled=True),
-        lax.all_gather(hid_share, "col", axis=0, tiled=True),
+        jnp.concatenate(
+            lax.all_to_all(jnp.stack([hid_share] * lax.axis_size("col")), "col", 0, 0), axis=0
+        ),
     )
     grad_w_out = lax.dot_general(
         activ_all, out_grad, (((0,), (0,)), ((), ())), preferred_element_type=jnp.float32

time: 242 us -> 216 us (0.89)
  waiting for transfers between devices: 196 us -> 166 us
  starting transfers between devices: 0.16 us -> 5.09 us
    all_gather x1 -> x0, waiting for transfers between devices: 37.7 us -> none  [per_device(): lax.all_gather(hid_share, 'col', axis=0, tiled=True)]
    all_to_all x0 -> x1, waiting for transfers between devices: none -> 30.3 us  [per_device(): lax.all_to_all(jnp.stack([hid_share] * lax.axis_size('col')), 'col', 0, 0)]
    all_gather x1, waiting for transfers between devices: 22.2 us -> 0.01 us  [per_device(): lax.all_gather(local_act.astype(jnp.bfloat16), 'col', axis=0, tiled=True)]
    all_to_all x0 -> x1, starting transfers between devices: none -> 4.97 us  [per_device(): lax.all_to_all(jnp.stack([hid_share] * lax.axis_size('col')), 'col', 0, 0)]
    unnamed x7 -> x5, local copies, waits for them, and re-layouts: 7.13 us -> 5.89 us
  transfers between devices with their start and end apart: 4 -> 4, of which waited for: 4 -> 3; matrix products, arithmetic and copies ran while one was open for 8% -> 9% of each run, Pallas kernels for 0% -> 0%
where the time goes in v1:
time: 216 us; the launch traced here: 215 us
  waiting for transfers between devices  166 us (77%)
  matrix products  20.7 us (10%)
  between operations  13.8 us (6%)
  local copies, waits for them, and re-layouts  6.98 us (3%)
  starting transfers between devices  5.09 us (2%)
  other arithmetic  3.39 us (2%)
    reduce_scatter x1, waiting for transfers between devices, per_device(): lax.psum_scatter(lax.dot_general(block, w_in, (((1,), (1,)), ((), ())), p...  88.2 us
    reduce_scatter x1, waiting for transfers between devices, per_device(): lax.psum_scatter(lax.dot_general(block, w_out, (((1,), (1,)), ((), ())),...  46.3 us
    all_to_all x1, waiting for transfers between devices, per_device(): lax.all_to_all(jnp.stack([hid_share] * lax.axis_size('col')), 'col', 0, 0)  30.3 us
    unnamed x5, local copies, waits for them, and re-layouts  5.89 us
    dot_general x1, matrix products, per_device(): lax.dot_general(block, w_in, (((1,), (1,)), ((), ())), preferred_element_...  5.82 us
    dot_general x1, matrix products, per_device(): lax.dot_general(inputs, hid_all, (((0,), (0,)), ((), ())), preferred_elem...  5.12 us
    dot_general x1, matrix products, per_device(): lax.dot_general(block, w_out, (((1,), (1,)), ((), ())), preferred_element...  5.09 us
    all_to_all x1, starting transfers between devices, per_device(): lax.all_to_all(jnp.stack([hid_share] * lax.axis_size('col')), 'col', 0, 0)  4.97 us
  transfers between devices with their start and end apart: 4, of which 3 were waited for; matrix products, arithmetic and copies ran while one was open for 9% of the time, Pallas kernels for 0%

profile of v1, /device:TPU:2, one launch (start us, length us, event | category | flops | bytes accessed | tf_op | source)
XLA Modules:
  0.0 215.5 jit_solution(4363516967143983496)
XLA Ops:
  7.2 0.0 copy-start
  7.2 0.0 reduce-scatter.3.cloned.1.call-start
  7.2 1.6 copy-done
  8.8 5.1 %fusion.12 = f32[768,768]{1,0:T(8,128)} fusion(bf16[768,1536]{1,0:T(8,128)(2,1)S(1)} %copy-done, bf16[768,1536]{1,0:T(8,128)(2,1)} %param.9), kind=kOutput, calls=%fused_computation.21 | convolution fusion | flops 1811939328 | bytes 7077888 | tf_op jit(solution)/shard_map/dot_general | solution.py:25
  13.9 0.0 copy-start.1
  13.9 0.0 reduce-scatter.3.cloned.1.call-update
  13.9 46.3 %reduce-scatter.3.cloned.1.call-done = f32[96,768]{1,0:T(8,128)} async-done(((f32[768,768]{1,0:T(8,128)}), f32[96,768]{1,0:T(8,128)}) %reduce-scatter.3.cloned.1.call-update) | async-done | bytes 294928 | tf_op jit(solution)/shard_map/reduce_scatter | solution.py:24
  60.3 0.0 copy-done.1
  60.3 1.8 fusion.8
  62.1 1.1 stack.2
  63.2 5.0 %all-to-all-start = ((bf16[8,96,768]{2,1,0:T(8,128)(2,1)}), bf16[8,96,768]{2,1,0:T(8,128)(2,1)S(1)}, u32[]{:S(2)}, u32[]{:S(2)}) async-start(bf16[8,96,768]{2,1,0:T(8,128)(2,1)} %stack.2), calls=%async_computation.1 | async-start | bytes 2359296 | tf_op jit(solution)/shard_map/all_to_all | solution.py:35
  68.2 0.0 all-gather.2.cloned.1.call-start
  68.2 0.7 all-gather.2.cloned.1.call-update
  68.9 0.0 reduce-scatter.5.cloned.1.call-start
  69.0 30.3 %all-to-all-done = bf16[8,96,768]{2,1,0:T(8,128)(2,1)S(1)} async-done(((bf16[8,96,768]{2,1,0:T(8,128)(2,1)}), bf16[8,96,768]{2,1,0:T(8,128)(2,1)S(1)}, u32[]{:S(2)}, u32[]{:S(2)}) %all-to-all-start) | async-done | bytes 1179680 | tf_op jit(solution)/shard_map/all_to_all | solution.py:35
  99.3 5.8 %fusion.13 = f32[768,1536]{1,0:T(8,128)} fusion(bf16[768,768]{1,0:T(8,128)(2,1)S(1)} %bitcast.11, bf16[1536,768]{1,0:T(8,128)(2,1)} %param.8), kind=kOutput, calls=%fused_computation.22 | convolution fusion | flops 1811939328 | bytes 8257536 | tf_op jit(solution)/shard_map/dot_general | solution.py:48
  105.1 0.0 reduce-scatter.5.cloned.1.call-update
  105.2 5.1 %fusion = bf16[1536,768]{0,1:T(8,128)(2,1)} fusion(bf16[768,768]{1,0:T(8,128)(2,1)S(1)} %bitcast.12, bf16[768,1536]{1,0:T(8,128)(2,1)} %param.5), kind=kOutput, calls=%fused_computation.2 | convolution fusion | flops 1814298624 | bytes 5898240 | tf_op jit(solution)/shard_map/dot_general | solution.py:42
  110.3 4.3 %copy.8 = bf16[1536,768]{1,0:T(8,128)(2,1)} copy(bf16[1536,768]{0,1:T(8,128)(2,1)} %fusion) | data formatting | bytes 4718592
  114.6 0.0 all-gather.2.cloned.1.call-done
  114.6 4.7 %multiply_convert_fusion = bf16[768,1536]{1,0:T(8,128)(2,1)} fusion(bf16[768,768]{1,0:T(8,128)(2,1)} %all-gather.2.cloned.1.call-done, bf16[768,1536]{1,0:T(8,128)(2,1)S(1)} %copy-done), kind=kOutput, calls=%fused_computation | convolution fusion | flops 1814298624 | bytes 5898240 | tf_op jit(solution)/shard_map/dot_general | solution.py:38
  119.3 88.2 %reduce-scatter.5.cloned.1.call-done = f32[24,1536]{1,0:T(8,128)} async-done(((f32[768,1536]{1,0:T(8,128)}), f32[24,1536]{1,0:T(8,128)}) %reduce-scatter.5.cloned.1.call-update) | async-done | bytes 147472 | tf_op jit(solution)/shard_map/reduce_scatter | solution.py:47
  207.4 1.6 convert_element_type.23
Async XLA Ops:
  7.2 1.7 copy-start
  7.2 53.1 %reduce-scatter.3.cloned.1.call-start = ((), (), s32[]{:S(2)}) async-start(), calls=%async_computation.3 | async-start | bytes 2654208 | tf_op jit(solution)/shard_map/reduce_scatter | solution.py:24
  13.9 46.3 %copy-start.1 = (bf16[96,768]{1,0:T(8,128)(2,1)S(1)}, bf16[96,768]{1,0:T(8,128)(2,1)}, u32[]{:S(2)}) copy-start(bf16[96,768]{1,0:T(8,128)(2,1)} %param.7) | copy-start | bytes 442372
  63.2 36.1 %all-to-all-start = ((bf16[8,96,768]{2,1,0:T(8,128)(2,1)}), bf16[8,96,768]{2,1,0:T(8,128)(2,1)S(1)}, u32[]{:S(2)}, u32[]{:S(2)}) async-start(bf16[8,96,768]{2,1,0:T(8,128)(2,1)} %stack.2), calls=%async_computation.1 | async-start | bytes 2359296 | tf_op jit(solution)/shard_map/all_to_all | solution.py:35
  68.2 46.4 %all-gather.2.cloned.1.call-start = ((), (), s32[]{:S(2)}) async-start(), calls=%async_computation.5 | async-start | bytes 1327104 | tf_op jit(solution)/shard_map/all_gather | solution.py:33
  68.9 138.5 %reduce-scatter.5.cloned.1.call-start = ((), (), s32[]{:S(2)}) async-start(), calls=%async_computation.4 | async-start | bytes 4866048 | tf_op jit(solution)/shard_map/reduce_scatter | solution.py:47
Sparse Core Ops, SparseCore 0:
  14.1 46.1 reduce-scatter.2
  70.8 42.5 all-gather.1
  117.4 89.9 reduce-scatter.4
